TPU v7x, 512 devices: a whole 4x4x16 slice. The times are simulated.
512 devices in a mesh: seq: 128 (over z, y, core), head: 4 (over x).
Axes of the slice: x: 4, y: 4, z: 16, core: 2. Of those that a mesh axis runs over, the one named last changes fastest.
Arguments:
- queries: bfloat16 [49152, 1536], P('seq', 'head'), may hold values from -34.5 to 34.5
- out_grad: bfloat16 [49152, 1536], P('seq', 'head'), may hold values from -48 to 48
- tile_mask: int32 [384, 2], P('seq'), may hold values from 0 to 1, as said below
- slot_caption: int32 [128, 2], replicated, may hold values from 0 to 32, as said below
- caption_cache: bfloat16 [2, 256, 512, 1536], P(None, 'seq', None, 'head'), may hold values from -6.1 to 6.1, as said below
- key_weight: bfloat16 [1536, 1536], P(None, 'head'), may hold values from -0.15625 to 0.15625
- value_weight: bfloat16 [1536, 1536], P(None, 'head'), may hold values from -0.15625 to 0.15625
Outputs:
- query_grad: bfloat16 [49152, 1536], P('seq', 'head')
- text_grad: bfloat16 [32, 512, 1536], P(None, 'seq', 'head')
Inputs may be any that keep to these rules, and one draw needn't show every extreme that they name: `tile_mask`: each row has exactly one 1; it marks the slot of its seq index whose caption the tile reads. `slot_caption`: row d lists the captions that the tiles of seq index d read, each once; one entry always names a caption, the other names another caption or is 32 for an empty slot, and no tile points to an empty slot. A caption's tiles are consecutive and lie on consecutive seq indices; a seq index holds at most one caption boundary; every caption is read. `caption_cache`: slots that hold the same caption hold equal copies of its keys and values.
All inputs are finite; a program needn't handle non-finite values.
Results may differ from a plain program's by a relative error of at most 0.0096.
Values may be sent and summed in bfloat16 or wider, within the bound.
A program may use at most 64 MiB of HBM per device.

v0:
```python
import math

import jax
import jax.numpy as jnp
from jax import lax
from jax.sharding import PartitionSpec as P

D = 1536
DH = 128
L = 512
TILE = 128
SPAN = 4


def shards(queries, out_grad, tile_mask, slot_caption, caption_cache, key_weight, value_weight):
    highest = lax.Precision.HIGHEST
    rows_here, width = queries.shape
    head_count = width // DH
    tile_count = rows_here // TILE
    slot_count = tile_mask.shape[1]
    inv_root = 1.0 / math.sqrt(DH)
    query_tiles = queries.reshape(tile_count, TILE, head_count, DH)
    grad_tiles = out_grad.reshape(tile_count, TILE, head_count, DH)
    slot_onehot = tile_mask.astype(jnp.float32)
    slot_lo = tile_mask.astype(jnp.bfloat16)
    key_rows = jnp.einsum(
        "ts,sjc->tjc", slot_lo, caption_cache[0], preferred_element_type=jnp.float32
    )
    key_rows = key_rows.astype(jnp.bfloat16).reshape(tile_count, L, head_count, DH)
    value_rows = jnp.einsum(
        "ts,sjc->tjc", slot_lo, caption_cache[1], preferred_element_type=jnp.float32
    )
    value_rows = value_rows.astype(jnp.bfloat16).reshape(tile_count, L, head_count, DH)
    scores = (
        jnp.einsum("tqhe,tjhe->thqj", query_tiles, key_rows, preferred_element_type=jnp.float32)
        * inv_root
    )
    row_max = jnp.max(scores, axis=-1, keepdims=True)
    exp_scores = jnp.exp(scores - row_max)
    attention = exp_scores / jnp.sum(exp_scores, axis=-1, keepdims=True)
    attention_lo = attention.astype(jnp.bfloat16)
    context = jnp.einsum(
        "thqj,tjhe->tqhe", attention_lo, value_rows, preferred_element_type=jnp.float32
    )
    row_dot = jnp.transpose(jnp.sum(grad_tiles.astype(jnp.float32) * context, axis=-1), (0, 2, 1))
    attention_grad = jnp.einsum(
        "tqhe,tjhe->thqj", grad_tiles, value_rows, preferred_element_type=jnp.float32
    )
    score_grad = attention * (attention_grad - row_dot[..., None])
    score_lo = score_grad.astype(jnp.bfloat16)
    query_grad = (
        jnp.einsum("thqj,tjhe->tqhe", score_lo, key_rows, preferred_element_type=jnp.float32)
        * inv_root
    )
    query_grad = query_grad.astype(jnp.bfloat16).reshape(rows_here, width)
    key_pieces = (
        jnp.einsum("thqj,tqhe->tjhe", score_lo, query_tiles, preferred_element_type=jnp.float32)
        * inv_root
    )
    value_pieces = jnp.einsum(
        "thqj,tqhe->tjhe", attention_lo, grad_tiles, preferred_element_type=jnp.float32
    )
    key_part = jnp.einsum("ts,tjhe->sjhe", slot_onehot, key_pieces, precision=highest)
    key_part = key_part.astype(jnp.bfloat16).reshape(slot_count, L, width)
    value_part = jnp.einsum("ts,tjhe->sjhe", slot_onehot, value_pieces, precision=highest)
    value_part = value_part.astype(jnp.bfloat16).reshape(slot_count, L, width)
    seq_count = lax.axis_size("seq")
    caption_count = seq_count // SPAN
    block_rows = L // seq_count
    flat_table = slot_caption.T.reshape(1, slot_count * seq_count)
    selector = (flat_table == jnp.arange(caption_count, dtype=jnp.int32)[:, None]).astype(
        jnp.float32
    )
    text_part = jnp.einsum(
        "mc,dc->md",
        key_part.reshape(slot_count * L, width),
        key_weight,
        preferred_element_type=jnp.float32,
    )
    text_part = text_part + jnp.einsum(
        "mc,dc->md",
        value_part.reshape(slot_count * L, width),
        value_weight,
        preferred_element_type=jnp.float32,
    )
    outgoing = text_part.reshape(slot_count, seq_count, block_rows, D)
    received = lax.all_to_all(outgoing, "seq", split_axis=1, concat_axis=1, tiled=True)
    summed = jnp.dot(
        selector, received.reshape(slot_count * seq_count, block_rows * D), precision=highest
    )
    summed = summed.reshape(caption_count, block_rows, D)
    text_grad = lax.psum_scatter(summed, "head", scatter_dimension=2, tiled=True).astype(
        jnp.bfloat16
    )
    return (query_grad, text_grad)


def solution(mesh):
    placed = (
        P("seq", "head"),
        P("seq", "head"),
        P("seq", None),
        P(),
        P(None, "seq", None, "head"),
        P(None, "head"),
        P(None, "head"),
    )
    return jax.shard_map(
        shards,
        mesh=mesh,
        in_specs=placed,
        out_specs=(P("seq", "head"), P(None, "seq", "head")),
        check_vma=False,
    )
```

profile of v0, /device:TPU:1, one launch (start us, length us, event | category | flops | bytes accessed | tf_op | source)
XLA Modules:
  0.0 434.8 jit_solution(16827312994940329809)
XLA Ops:
  7.2 1.4 reshape.33
  8.6 1.4 reshape.35
  11.0 1.5 fusion.55
  12.6 3.4 convolution_convert_fusion
  16.0 3.5 copy.64
  19.5 3.4 convolution_convert_fusion.1
  23.0 2.6 copy.60
  26.1 2.1 fusion.56
  28.2 4.8 %convolution_bitcast_fusion = f32[3,512,3,128]{3,1,2,0:T(8,128)} fusion(bf16[3,128,3,128]{1,3,2,0:T(8,128)(2,1)} %copy.67, f32[3,3,128]{2,1,0:T(4,128)S(1)} %get-tuple-element.12, f32[3,3,512,128]{3,2,1,0:T(8,128)} %copy-done.2), kind=kOutput, calls=%fused_computation.14 | convolution fusion | flops 153945728 | bytes 5018112 | tf_op jit(solution)/shard_map/thqj,tqhe->tjhe/dot_general | solution.py:60
  33.0 4.1 fusion.25
  37.2 9.5 %fusion.17 = bf16[2,512,3,128]{3,0,2,1:T(2,128)(2,1)} fusion(f32[3,512,3,128]{3,1,2,0:T(8,128)} %convolution_bitcast_fusion, s32[3,2]{0,1:T(2,128)S(1)} %copy-done.8), kind=kOutput, calls=%fused_computation.19 | convolution fusion | flops 14548998 | bytes 3145752 | tf_op jit(solution)/shard_map/ts,tjhe->sjhe/dot_general | solution.py:65
  46.6 2.9 copy.76
  50.6 2.8 fusion.5
  53.9 8.4 %fusion.20 = bf16[2,512,3,128]{3,0,2,1:T(2,128)(2,1)} fusion(f32[3,512,3,128]{3,1,2,0:T(8,128)S(1)} %multiply_bitcast_fusion, s32[3,2]{0,1:T(2,128)S(1)} %copy-done.8), kind=kOutput, calls=%fused_computation.20 | convolution fusion | flops 14548998 | bytes 3145752 | tf_op jit(solution)/shard_map/ts,tjhe->sjhe/dot_general | solution.py:63
  62.3 3.8 copy.73
  67.4 1.9 fusion.57
  69.3 4.5 %convolution_add_fusion = f32[1024,1536]{1,0:T(8,128)} fusion(f32[1024,1536]{1,0:T(8,128)S(1)} %fusion.57, bf16[1024,384]{0,1:T(8,128)(2,1)S(1)} %bitcast.114, bf16[1536,384]{1,0:T(8,128)(2,1)S(1)} %copy-done.6), kind=kOutput, calls=%fused_computation.1 | convolution fusion | flops 1209532416 | bytes 14548992 | tf_op jit(solution)/shard_map/mc,dc->md/dot_general | solution.py:80
  73.8 7.6 %reshape.37 = f32[2,128,4,1536]{3,2,1,0:T(4,128)} reshape(f32[1024,1536]{1,0:T(8,128)} %convolution_add_fusion) | data formatting | bytes 12582912 | tf_op jit(solution)/shard_map/reshape | solution.py:86
  81.3 5.0 %copy.77 = f32[2,128,4,1536]{3,2,0,1:T(4,128)S(1)} copy(f32[2,128,4,1536]{3,2,1,0:T(4,128)} %reshape.37) | data formatting | bytes 12582912 | tf_op jit(solution)/shard_map/reshape | solution.py:86
  86.3 296.7 %all_to_all.5 = f32[2,128,4,1536]{3,2,0,1:T(4,128)S(1)} all-to-all(f32[2,128,4,1536]{3,2,0,1:T(4,128)S(1)} %copy.77), channel_id=1, replica_groups=mesh['seq'=128,'head'=4] {'seq'}, dimensions={1} | all-to-all | bytes 12582912 | tf_op jit(solution)/shard_map/all_to_all | solution.py:87
  384.1 5.2 %copy.91 = f32[32,8,4,1536]{3,1,2,0:T(8,128)} copy(f32[32,8,4,1536]{3,2,1,0:T(4,128)S(1)} %bitcast.108) | data formatting | bytes 12582912
  389.4 6.6 %copy.79 = f32[6144,256]{1,0:T(8,128)} copy(f32[6144,256]{0,1:T(8,128)} %bitcast.109) | data formatting | bytes 12582912 | tf_op jit(solution)/shard_map/dot_general | solution.py:88
  396.0 6.8 %fusion.33 = f32[32,4,1536]{2,0,1:T(8,128)} fusion(f32[4,1536,256]{2,1,0:T(8,128)} %bitcast.110, s32[256]{0:T(256)S(1)} %bitcast.121), kind=kOutput, calls=%fused_computation.38 | convolution fusion | flops 603987968 | bytes 7078912 | tf_op jit(solution)/shard_map/dot_general | solution.py:88
  406.0 20.3 %reduce-scatter.2.cloned.1.call-done = f32[32,4,384]{2,0,1:T(8,128)} async-done(((f32[32,4,1536]{2,0,1:T(8,128)}), f32[32,4,384]{2,0,1:T(8,128)}) %reduce-scatter.2.cloned.1.call-update) | async-done | bytes 196624 | tf_op jit(solution)/shard_map/reduce_scatter | solution.py:92
  (33 shorter events, 10.3 us)
Async XLA Ops:
  7.2 60.2 %copy-start = (bf16[1536,384]{1,0:T(8,128)(2,1)S(1)}, bf16[1536,384]{1,0:T(8,128)(2,1)}, u32[]{:S(2)}) copy-start(bf16[1536,384]{1,0:T(8,128)(2,1)} %param.12) | copy-start | bytes 3538948
  7.2 419.2 %reduce-scatter.2.cloned.1.call-start = ((), (), s32[]{:S(2)}) async-start(), calls=%async_computation.2 | async-start | bytes 983040 | tf_op jit(solution)/shard_map/reduce_scatter | solution.py:92
  8.6 16.9 %copy-start.4 = (bf16[3,128,3,128]{3,2,1,0:T(4,128)(2,1)}, bf16[3,128,3,128]{3,2,1,0:T(4,128)(2,1)S(1)}, u32[]{:S(2)}) copy-start(bf16[3,128,3,128]{3,2,1,0:T(4,128)(2,1)S(1)} %reshape.33) | copy-start | bytes 884740
  8.6 3.9 copy-start.8
  26.1 2.1 copy-start.2
  28.2 4.8 %copy-start.7 = (bf16[3,512,384]{1,2,0:T(8,128)(2,1)S(1)}, bf16[3,512,384]{1,2,0:T(8,128)(2,1)}, u32[]{:S(2)}) copy-start(bf16[3,512,384]{1,2,0:T(8,128)(2,1)} %copy.64) | copy-start | bytes 3538948
  50.6 2.8 copy-start.5
  67.4 1.9 copy-start.3
  67.4 1.9 copy-start.6
  389.4 6.6 %copy-start.9 = (s32[128,2]{0,1:T(2,128)S(1)}, s32[128,2]{0,1:T(2,128)}, u32[]{:S(2)}) copy-start(s32[128,2]{0,1:T(2,128)} %param.10) | copy-start | bytes 3076
  402.9 25.1 %copy-start.1 = (bf16[1536,384]{1,0:T(8,128)(2,1)S(1)}, bf16[1536,384]{1,0:T(8,128)(2,1)}, u32[]{:S(2)}) copy-start(bf16[1536,384]{1,0:T(8,128)(2,1)} %param.12) | copy-start | bytes 3538948
Sparse Core Ops, SparseCore 0:
  403.0 23.3 reduce-scatter.1
where the time goes:
time: 437 us; the launch traced here: 435 us
  blocking collectives  297 us (68%)
  matrix products  51.9 us (12%)
  local copies, waits for them, and re-layouts  48.6 us (11%)
  waiting for transfers between devices  20.3 us (5%)
  between operations  14.2 us (3%)
    all_to_all x1, blocking collectives, shards(): lax.all_to_all(outgoing, 'seq', split_axis=1, concat_axis=1, tiled=True)  297 us
    reduce_scatter x1, waiting for transfers between devices, shards(): lax.psum_scatter(summed, 'head', scatter_dimension=2, tiled=True)  20.3 us
    reshape x2, local copies, waits for them, and re-layouts, shards(): outgoing = text_part.reshape(slot_count, seq_count, block_rows, D)  12.5 us
    dot_general x1, matrix products, shards(): jnp.einsum('ts,tjhe->sjhe', slot_onehot, value_pieces, precision=highest)  9.46 us
    unnamed x25, local copies, waits for them, and re-layouts  9.05 us
  transfers between devices with their start and end apart: 1, of which 1 were waited for; matrix products, arithmetic and copies ran while one was open for 1% of the time, Pallas kernels for 0%

commit v1 on v0

v1 whole, which is shorter than its diff:
```python
import functools
import math

import jax
import jax.numpy as jnp
from jax import lax
from jax.experimental import pallas as pl
from jax.experimental.pallas import tpu as pltpu
from jax.sharding import PartitionSpec as P

DH = 128
L = 512
TILE = 128
NT = 3
NH = 3
NX = 4
NY = 4
NZ = 16
NC = 2
ROWS = 4
GROUP = 4
CAPS = 32
HD = NH * DH
INV_ROOT = 1.0 / math.sqrt(DH)
MESH = pl.DeviceIdType.MESH
F32 = jnp.float32
BF16 = jnp.bfloat16
NT_DIMS = (((1,), (1,)), ((), ()))
TN_DIMS = (((0,), (0,)), ((), ()))
ORDER = [NZ // 2 + j // 2 if j % 2 == 0 else NZ // 2 - (j + 1) // 2 for j in range(NZ)]


def one_hot(rows, columns):
    return jnp.where(rows == columns, 1.0, 0.0).astype(BF16)


def kernel(
    meta, capcol, q_hbm, g_hbm, cache_hbm, kw_hbm, vw_hbm,
    qg_hbm, text_ref, parts_hbm,
    q_v, g_v, raw, kvp, w_v, qg_v, ds_s, at_s, parts, prx, pm, yrx, x_s, tsend, xrx, town, zsend, zrx,
    load_sem, store_sem, ps, pr, ys, yr, xs, xr, zs, zr,
):
    seq = lax.axis_index("seq")
    x = lax.axis_index("head")
    core = lax.rem(seq, 2)
    y = lax.rem(seq // 2, NY)
    z = seq // (2 * NY)

    def seq_of(z_, y_, core_):
        return (z_ * NY + y_) * 2 + core_

    pair_id = (seq_of(z, y, 1 - core), x)
    y_ids = [(seq_of(z, lax.rem(y + k, NY), core), x) for k in range(1, NY)]
    x_ids = [(seq, lax.rem(x + k, NX)) for k in range(1, NX)]
    z_ids = [(seq_of(lax.rem(z + k, NZ), y, core), x) for k in ORDER[:-1]]

    loads = []
    for kv in range(2):
        for s in range(2):
            loads.append(
                pltpu.make_async_copy(cache_hbm.at[kv, s], raw.at[kv, s], load_sem.at[kv * 2 + s])
            )
    loads.append(pltpu.make_async_copy(q_hbm, q_v, load_sem.at[4]))
    loads.append(pltpu.make_async_copy(g_hbm, g_v, load_sem.at[5]))
    loads.append(pltpu.make_async_copy(kw_hbm, w_v.at[0], load_sem.at[6]))
    loads.append(pltpu.make_async_copy(vw_hbm, w_v.at[1], load_sem.at[7]))
    for load in loads:
        load.start()

    barrier = pltpu.get_barrier_semaphore()
    partners = [pair_id] + y_ids + x_ids + z_ids
    for partner in partners:
        pl.semaphore_signal(barrier, inc=1, device_id=partner, device_id_type=MESH)

    n = lax.broadcasted_iota(jnp.int32, (L, L), 0)
    place = (n >> 2) & (NZ - 1)
    half = place >> 1
    dist = jnp.where((place & 1) == 0, NZ // 2 + half, NZ // 2 - 1 - half)
    zdest = (z + dist) & (NZ - 1)
    old = zdest * 32 + ((n >> 6) & 3) * 8 + (n >> 8) * 4 + (n & 3)
    perm = one_hot(old, lax.broadcasted_iota(jnp.int32, (L, L), 1))
    for kv in range(2):
        for s in range(2):
            loads[kv * 2 + s].wait()
            moved = jnp.dot(perm, raw[kv, s], preferred_element_type=F32).astype(BF16)
            for h in range(NH):
                kvp[s, h, :, kv * DH : (kv + 1) * DH] = moved[:, h * DH : (h + 1) * DH]
    loads[4].wait()
    loads[5].wait()

    def pair_copy(h):
        return pltpu.make_async_remote_copy(
            src_ref=parts.at[h, 1 - core], dst_ref=prx.at[h],
            send_sem=ps.at[h], recv_sem=pr.at[h],
            device_id=pair_id, device_id_type=MESH,
        )

    def y_copy(h, k, source):
        return pltpu.make_async_remote_copy(
            src_ref=pm.at[h, lax.rem(y + k, NY)], dst_ref=yrx.at[h, source],
            send_sem=ys.at[h, k - 1], recv_sem=yr.at[h, k - 1],
            device_id=y_ids[k - 1], device_id_type=MESH,
        )

    def x_copy(k, c):
        return pltpu.make_async_remote_copy(
            src_ref=tsend.at[k - 1, c], dst_ref=xrx.at[k - 1, c],
            send_sem=xs.at[k - 1, c], recv_sem=xr.at[k - 1, c],
            device_id=x_ids[k - 1], device_id_type=MESH,
        )

    def z_copy(j, source):
        return pltpu.make_async_remote_copy(
            src_ref=zsend.at[j], dst_ref=zrx.at[source],
            send_sem=zs.at[j], recv_sem=zr.at[j],
            device_id=z_ids[j], device_id_type=MESH,
        )

    def attend(h, t):
        rows = slice(t * TILE, (t + 1) * TILE)
        cols = slice(h * DH, (h + 1) * DH)
        kv = kvp[meta[t], h]
        q = q_v[rows, cols]
        g = g_v[rows, cols]
        zero = jnp.zeros_like(q)
        both = jnp.concatenate(
            [jnp.concatenate([q, zero], axis=1), jnp.concatenate([zero, g], axis=1)], axis=0
        )
        res = lax.dot_general(kv, both, NT_DIMS, preferred_element_type=F32)
        scores = res[:, :TILE] * INV_ROOT
        grads = res[:, TILE:]
        e = jnp.exp(scores - jnp.max(scores, axis=0, keepdims=True))
        att = e * (1.0 / jnp.sum(e, axis=0, keepdims=True))
        att_lo = att.astype(BF16)
        row_dot = jnp.sum(att_lo.astype(F32) * grads, axis=0, keepdims=True)
        ds = (att * (grads - row_dot)).astype(BF16)
        at_s[h, :, rows] = att_lo
        ds_s[h, :, rows] = ds
        qg = lax.dot_general(ds, kv[:, :DH], TN_DIMS, preferred_element_type=F32) * INV_ROOT
        qg_v[rows, cols] = qg.astype(BF16)

    def masked(ref, h):
        tiles = []
        for t in range(NT):
            v = ref[t * TILE : (t + 1) * TILE, h * DH : (h + 1) * DH].astype(F32)
            ranks = [v * meta[NT + 2 * t + r].astype(F32) for r in range(2)]
            tiles.append(jnp.concatenate(ranks, axis=1).astype(BF16))
        return jnp.concatenate(tiles, axis=0)

    def reduce_rows(h):
        key = jnp.dot(ds_s[h], masked(q_v, h), preferred_element_type=F32) * INV_ROOT
        value = jnp.dot(at_s[h], masked(g_v, h), preferred_element_type=F32)
        for hf in range(2):
            parts[h, hf, 0] = key[hf * 256 : (hf + 1) * 256].astype(BF16)
            parts[h, hf, 1] = value[hf * 256 : (hf + 1) * 256].astype(BF16)

    def merge_pair(h):
        pair_copy(h).wait_recv()
        total = (parts[h, core].astype(F32) + prx[h].astype(F32)).astype(BF16)
        for b in range(NY):
            pm[h, b] = total[:, b * 64 : (b + 1) * 64, :]
        for k in (2, 1, 3):
            y_copy(h, k, y).start()
        yrx[h, y] = pm[h, y]

    stores = []
    for h in range(NH):
        for t in range(NT):
            attend(h, t)
            if h > 0 and t == 1:
                merge_pair(h - 1)
        reduce_rows(h)
        if h == 0:
            pl.semaphore_wait(barrier, len(partners))
        pair_copy(h).start()
        store = pltpu.make_async_copy(parts.at[h], parts_hbm.at[h], store_sem.at[h])
        store.start()
        stores.append(store)
    store = pltpu.make_async_copy(qg_v, qg_hbm, store_sem.at[NH])
    store.start()
    stores.append(store)
    merge_pair(NH - 1)

    loads[6].wait()
    loads[7].wait()
    for h in range(NH):
        for k in (1, 3, 2):
            y_copy(h, k, lax.rem(y + NY - k, NY)).wait_recv()
        for gp in range(2):
            total = (yrx[h, 2 * gp].astype(F32) + yrx[h, 2 * gp + 1].astype(F32)).astype(BF16)
            for p in range(2):
                for kv in range(2):
                    x_s[
                        (gp * 2 + p) * 64 : (gp * 2 + p + 1) * 64,
                        kv * HD + h * DH : kv * HD + (h + 1) * DH,
                    ] = total[kv, :, p * DH : (p + 1) * DH]

    n = lax.broadcasted_iota(jnp.int32, (256, 256), 0)
    old = ((n >> 2) & 3) * 64 + (n >> 4) * 4 + (n & 3)
    perm = one_hot(old, lax.broadcasted_iota(jnp.int32, (256, 256), 1))
    joined = jnp.dot(perm, x_s[...], preferred_element_type=F32).astype(BF16)
    chunk = 256 // NC
    places = NZ // NC

    def project(c, target):
        piece = joined[c * chunk : (c + 1) * chunk]
        return lax.dot_general(
            piece[:, :HD], w_v[0, target], NT_DIMS, preferred_element_type=F32
        ) + lax.dot_general(piece[:, HD:], w_v[1, target], NT_DIMS, preferred_element_type=F32)

    for c in range(NC):
        for k in (2, 1, 3):
            tsend[k - 1, c] = project(c, lax.rem(x + k, NX)).astype(BF16)
            x_copy(k, c).start()
    for c in range(NC):
        town[c] = project(c, x)
    for c in range(NC):
        total = town[c]
        for k in (1, 3, 2):
            x_copy(k, c).wait_recv()
            total = total + xrx[k - 1, c].astype(F32)
        zsend[c * places : (c + 1) * places] = total.astype(BF16).reshape(places, 16, HD)
        for j in range(c * places, (c + 1) * places):
            if j < NZ - 1:
                z_copy(j, z).start()
    zrx[z] = zsend[NZ - 1]

    rows = lax.broadcasted_iota(jnp.int32, (CAPS * ROWS, 256), 0)
    cols = lax.broadcasted_iota(jnp.int32, (CAPS * ROWS, 256), 1)
    held = (capcol[...] == (rows >> 2)) & ((rows & 3) == (cols & 3))
    select = jnp.where(held, 1.0, 0.0).astype(BF16)
    for j in range(NZ - 1):
        z_copy(j, lax.rem(z + NZ - ORDER[j], NZ)).wait_recv()
    text = jnp.dot(select, zrx[...].reshape(256, HD), preferred_element_type=F32)
    text_ref[...] = text.astype(BF16)

    for h in range(NH):
        pair_copy(h).wait_send()
        for k in range(1, NY):
            y_copy(h, k, y).wait_send()
    for c in range(NC):
        for k in range(1, NX):
            x_copy(k, c).wait_send()
    for j in range(NZ - 1):
        z_copy(j, z).wait_send()
    for store in stores:
        store.wait()


def run(meta, capcol, queries, out_grad, cache, key_weight, value_weight):
    hbm = pl.BlockSpec(memory_space=pl.ANY)
    dma = pltpu.SemaphoreType.DMA
    return pl.pallas_call(
        kernel,
        out_shape=(
            jax.ShapeDtypeStruct((NT * TILE, HD), BF16),
            jax.ShapeDtypeStruct((CAPS * ROWS, HD), BF16),
            jax.ShapeDtypeStruct((NH, 2, 2, 256, 256), BF16),
        ),
        in_specs=[
            pl.BlockSpec(memory_space=pltpu.SMEM),
            pl.BlockSpec(memory_space=pltpu.VMEM),
            hbm, hbm, hbm, hbm, hbm,
        ],
        out_specs=(hbm, pl.BlockSpec(memory_space=pltpu.VMEM), hbm),
        scratch_shapes=[
            pltpu.VMEM((NT * TILE, HD), BF16),
            pltpu.VMEM((NT * TILE, HD), BF16),
            pltpu.VMEM((2, 2, L, HD), BF16),
            pltpu.VMEM((2, NH, L, 2 * DH), BF16),
            pltpu.VMEM((2, NX, HD, HD), BF16),
            pltpu.VMEM((NT * TILE, HD), BF16),
            pltpu.VMEM((NH, L, NT * TILE), BF16),
            pltpu.VMEM((NH, L, NT * TILE), BF16),
            pltpu.VMEM((NH, 2, 2, 256, 256), BF16),
            pltpu.VMEM((NH, 2, 256, 256), BF16),
            pltpu.VMEM((NH, NY, 2, 64, 256), BF16),
            pltpu.VMEM((NH, NY, 2, 64, 256), BF16),
            pltpu.VMEM((256, 2 * HD), BF16),
            pltpu.VMEM((NX - 1, NC, 256 // NC, HD), BF16),
            pltpu.VMEM((NX - 1, NC, 256 // NC, HD), BF16),
            pltpu.VMEM((NC, 256 // NC, HD), F32),
            pltpu.VMEM((NZ, 16, HD), BF16),
            pltpu.VMEM((NZ, 16, HD), BF16),
            dma((8,)),
            dma((NH + 1,)),
            dma((NH,)),
            dma((NH,)),
            dma((NH, NY - 1)),
            dma((NH, NY - 1)),
            dma((NX - 1, NC)),
            dma((NX - 1, NC)),
            dma((NZ - 1,)),
            dma((NZ - 1,)),
        ],
        compiler_params=pltpu.CompilerParams(
            collective_id=0, has_side_effects=True, vmem_limit_bytes=48 * 1024 * 1024
        ),
    )(
        meta, capcol, queries, out_grad, cache,
        key_weight.reshape(NX, HD, HD), value_weight.reshape(NX, HD, HD),
    )


def general(parts, slot_caption, key_weight, value_weight):
    z = lax.axis_index("seq") // (2 * NY)
    places = jnp.arange(NZ)
    dist = jnp.asarray(ORDER)
    order = jnp.argsort((z + dist) % NZ)
    split = parts.reshape(NH, 2, 2, NY, NZ, ROWS, 2, DH)[:, :, :, :, order]
    outgoing = split.transpose(4, 3, 1, 6, 5, 2, 0, 7).reshape(2 * NY * NZ, 2, ROWS * 2 * HD)
    received = lax.all_to_all(outgoing, "seq", split_axis=0, concat_axis=0, tiled=True)
    table = slot_caption.reshape(1, -1)
    selector = (table == jnp.arange(CAPS, dtype=jnp.int32)[:, None]).astype(BF16)
    summed = jnp.dot(selector, received.reshape(-1, ROWS * 2 * HD), preferred_element_type=F32)
    summed = summed.reshape(CAPS * ROWS, 2, HD)
    highest = lax.Precision.HIGHEST
    text = jnp.einsum("mc,dc->md", summed[:, 0], key_weight.astype(F32), precision=highest)
    text = text + jnp.einsum("mc,dc->md", summed[:, 1], value_weight.astype(F32), precision=highest)
    pieces = text.reshape(CAPS * ROWS, NX, HD).transpose(1, 0, 2)
    pieces = lax.all_to_all(pieces, "head", split_axis=0, concat_axis=0, tiled=True)
    return jnp.sum(pieces, axis=0).astype(BF16)


def shards(queries, out_grad, tile_mask, slot_caption, caption_cache, key_weight, value_weight):
    me = lax.axis_index("seq")
    groups = slot_caption.reshape(-1, GROUP * 2)
    live = groups < CAPS
    low = jnp.min(jnp.where(live, groups, CAPS), axis=1)
    high = jnp.max(jnp.where(live, groups, -1), axis=1)
    fits = jnp.all(~live | (groups == low[:, None]) | (groups == high[:, None]))
    held = jnp.stack([low, jnp.where(high > low, high, CAPS)], axis=1)
    capcol = jnp.repeat(held.reshape(1, -1), ROWS, axis=1)
    mine = lax.dynamic_slice(slot_caption, (me, 0), (1, 2))[0]
    rank = jnp.where(fits, (mine != low[me // GROUP]).astype(jnp.int32), jnp.arange(2, dtype=jnp.int32))
    mask = jnp.sum(
        tile_mask[:, :, None] * (rank[:, None] == jnp.arange(2, dtype=jnp.int32)[None, :]), axis=1
    )
    meta = jnp.concatenate([tile_mask[:, 1], mask.reshape(-1)]).astype(jnp.int32)
    query_grad, fast, parts = run(
        meta, capcol, queries, out_grad, caption_cache, key_weight, value_weight
    )
    text = lax.cond(
        fits,
        lambda f, p, s, k, v: f,
        lambda f, p, s, k, v: general(p, s, k, v),
        fast, parts, slot_caption, key_weight, value_weight,
    )
    return query_grad, text.reshape(CAPS, ROWS, HD)


def solution(mesh):
    placed = (
        P("seq", "head"),
        P("seq", "head"),
        P("seq", None),
        P(),
        P(None, "seq", None, "head"),
        P(None, "head"),
        P(None, "head"),
    )
    return jax.shard_map(
        shards,
        mesh=mesh,
        in_specs=placed,
        out_specs=(P("seq", "head"), P(None, "seq", "head")),
        check_vma=False,
    )
```

time: 437 us -> 65.2 us (0.15)
  blocking collectives: 297 us -> 0 us
  matrix products: 51.9 us -> 0 us
  Pallas kernels: 0 us -> 51.4 us
  local copies, waits for them, and re-layouts: 48.6 us -> 6.49 us
  waiting for transfers between devices: 20.3 us -> 0 us
  between operations: 14.2 us -> 1.39 us
    all_to_all x1 -> x0, blocking collectives: 297 us -> none  [shards(): lax.all_to_all(outgoing, 'seq', split_axis=1, concat_axis=1, tiled=True)]
    dot_general x13 -> x0, matrix products: 51.9 us -> none  [the longest x1 9.46 us: shards(): jnp.einsum('ts,tjhe->sjhe', slot_onehot, value_pieces, precision=highest)]
    pallas_call x0 -> x1, Pallas kernels: none -> 51.4 us  [run(): pl.pallas_call(kernel, out_shape=(jax.ShapeDtypeStruct((NT * TILE, HD), B...]
    reduce_scatter x1 -> x0, waiting for transfers between devices: 20.3 us -> none  [shards(): lax.psum_scatter(summed, 'head', scatter_dimension=2, tiled=True)]
    reshape x5 -> x3, local copies, waits for them, and re-layouts: 16.3 us -> 0.22 us  [the longest x1 0.1 us: shards(): capcol = jnp.repeat(held.reshape(1, -1), ROWS, axis=1)]
    convert_element_type x5 -> x0, local copies, waits for them, and re-layouts: 14 us -> none  [the longest x1 3.75 us: shards(): key_part = key_part.astype(jnp.bfloat16).reshape(slot_count, L, width)]
    dot_general x1 -> x0, local copies, waits for them, and re-layouts: 6.61 us -> none  [shards(): jnp.dot(selector, received.reshape(slot_count * seq_count, block_rows * D...]
    unnamed x25 -> x11, local copies, waits for them, and re-layouts: 9.05 us -> 4.07 us
  transfers between devices with their start and end apart: 1 -> 0, of which waited for: 1 -> 0; matrix products, arithmetic and copies ran while one was open for 1% -> 0% of each run, Pallas kernels for 0% -> 0%
where the time goes in v1:
time: 65.2 us; the launch traced here: 64.9 us
  Pallas kernels  51.4 us (79%)
  local copies, waits for them, and re-layouts  6.49 us (10%)
  other arithmetic  5.34 us (8%)
  between operations  1.39 us (2%)
    pallas_call x1, Pallas kernels, run(): pl.pallas_call(kernel, out_shape=(jax.ShapeDtypeStruct((NT * TILE, HD), B...  51.4 us
    unnamed x11, local copies, waits for them, and re-layouts  4.07 us
    convert_element_type x1, other arithmetic, shards(): (mine != low[me // GROUP]).astype(jnp.int32)  1.51 us
    reduce_and x1, other arithmetic, shards(): fits = jnp.all(~live | (groups == low[:, None]) | (groups == high[:, None]))  1.33 us

profile of v1, /device:TPU:1, one launch (start us, length us, event | category | flops | bytes accessed | tf_op | source)
XLA Modules:
  0.0 64.9 jit_solution(12450171149283332387)
XLA Ops:
  0.6 0.7 %fusion.13 = (s32[128]{0:T(128)S(1)}, s32[128]{0:T(128)S(1)}) fusion(s32[128,2]{0,1:T(2,128)} %param.13), kind=kLoop, calls=%fused_computation.29 | loop fusion | flops 1024 | bytes 2048 | tf_op jit(solution)/shard_map/reduce_max | solution.py:330
  1.3 0.1 reduce_min.14
  1.4 0.1 reduce_min.18
  1.6 0.6 dynamic_slice.7
  2.2 1.5 %fusion.11 = s32[2]{0:T(128)S(1)} fusion(s32[128,2]{0,1:T(2,128)} %param.13, s32[]{:T(128)S(6)} %select_n.58, s32[]{:T(128)} %bitcast.3), kind=kLoop, calls=%fused_computation.27 | loop fusion | flops 4 | bytes 24 | tf_op jit(solution)/shard_map/convert_element_type | solution.py:335
  3.7 0.1 reduce_max.15
  3.8 0.1 reduce_max.20
  4.0 0.1 eq.65
  4.2 0.1 eq.61
  4.3 1.3 %fusion.10 = pred[]{:T(512)} fusion(s32[128,2]{0,1:T(2,128)} %param.13, s32[128]{0:T(128)S(1)} %eq.65, s32[128]{0:T(128)S(1)} %eq.61), kind=kLoop, calls=%fused_computation.26 | loop fusion | flops 1791 | bytes 2049 | tf_op jit(solution)/shard_map/reduce_and | solution.py:331
  5.6 0.6 broadcast_select_fusion
  6.3 0.8 %multiply_reduce_fusion = s32[3,2]{0,1:T(2,128)S(1)} fusion(s32[2,2]{1,0:T(2,128)S(1)} %compare_convert_fusion, s32[3,2]{0,1:T(2,128)} %param.12), kind=kLoop, calls=%fused_computation.21 | loop fusion | flops 18 | bytes 64 | tf_op jit(solution)/shard_map/reduce_sum | solution.py:336
  7.1 0.1 copy.38
  7.2 0.1 reshape.102
  7.3 0.7 %slice_bitcast_fusion = s32[3]{0:T(128)S(1)} fusion(s32[3,2]{0,1:T(2,128)} %param.12), kind=kLoop, calls=%fused_computation.33 | loop fusion | bytes 24 | tf_op jit(solution)/shard_map/squeeze | solution.py:339
  8.0 0.1 copy.39
  8.1 0.1 reshape.103
  8.3 0.1 broadcast_in_dim.30.capcol
  8.4 1.4 %copy-done = bf16[2,2,512,384]{3,2,1,0:T(8,128)(2,1)S(1)} copy-done((bf16[2,2,512,384]{3,2,1,0:T(8,128)(2,1)S(1)}, bf16[2,2,512,384]{3,2,1,0:T(8,128)(2,1)}, u32[]{:S(2)}) %copy-start) | copy-done | bytes 1572888
  9.8 1.0 %copy-done.1 = bf16[384,384]{1,0:T(8,128)(2,1)S(1)} copy-done((bf16[384,384]{1,0:T(8,128)(2,1)S(1)}, bf16[384,384]{1,0:T(8,128)(2,1)}, u32[]{:S(2)}) %copy-start.1) | copy-done | bytes 294936
  10.8 1.0 %copy-done.2 = bf16[384,384]{1,0:T(8,128)(2,1)S(1)} copy-done((bf16[384,384]{1,0:T(8,128)(2,1)S(1)}, bf16[384,384]{1,0:T(8,128)(2,1)}, u32[]{:S(2)}) %copy-start.2) | copy-done | bytes 294936
  11.8 51.4 %shard_map.96 = (bf16[384,384]{1,0:T(8,128)(2,1)S(1)}, bf16[128,384]{1,0:T(8,128)(2,1)S(1)}, bf16[3,2,2,256,256]{4,3,2,1,0:T(8,128)(2,1)}) custom-call(s32[9]{0:T(128)S(1)} %pad_add_fusion.1.meta, s32[1,256]{1,0:T(1,128)S(1)} %broadcast_in_dim.30.capcol, bf16[384,384]{1,0:T(8,128)(2,1)S(1)} %copy-done.1, bf16[384,384]{1,0:T(8,128)(2,1)S(1)} %copy-done.2, ...), custom_call_target="tpu_custom_call" | custom-call | tf_op jit(solution)/shard_map/pallas_call | solution.py:253
  63.9 0.3 conditional.1
  64.1 0.7 %copy.59 = bf16[384,384]{1,0:T(8,128)(2,1)} copy(bf16[384,384]{1,0:T(8,128)(2,1)S(1)} %get-tuple-element.63) | data formatting | bytes 589824
  (15 shorter events, 0.4 us)
Async XLA Ops:
  8.4 1.4 %copy-start = (bf16[2,2,512,384]{3,2,1,0:T(8,128)(2,1)S(1)}, bf16[2,2,512,384]{3,2,1,0:T(8,128)(2,1)}, u32[]{:S(2)}) copy-start(bf16[2,2,512,384]{3,2,1,0:T(8,128)(2,1)} %cache_hbm.1) | copy-start | bytes 4718596
  9.8 1.0 %copy-start.1 = (bf16[384,384]{1,0:T(8,128)(2,1)S(1)}, bf16[384,384]{1,0:T(8,128)(2,1)}, u32[]{:S(2)}) copy-start(bf16[384,384]{1,0:T(8,128)(2,1)} %q_hbm.1) | copy-start | bytes 884740
  10.8 1.0 %copy-start.2 = (bf16[384,384]{1,0:T(8,128)(2,1)S(1)}, bf16[384,384]{1,0:T(8,128)(2,1)}, u32[]{:S(2)}) copy-start(bf16[384,384]{1,0:T(8,128)(2,1)} %g_hbm.1) | copy-start | bytes 884740
  11.8 52.1 %copy-start.6 = (s32[128,2]{0,1:T(2,128)S(1)}, s32[128,2]{0,1:T(2,128)}, u32[]{:S(2)}) copy-start(s32[128,2]{0,1:T(2,128)} %param.13) | copy-start | bytes 3076
  64.1 0.8 %copy-start.5 = (bf16[32,4,384]{2,1,0:T(4,128)(2,1)}, bf16[32,4,384]{2,1,0:T(4,128)(2,1)S(1)}, u32[]{:S(2)}) copy-start(bf16[32,4,384]{2,1,0:T(4,128)(2,1)S(1)} %get-tuple-element.65) | copy-start | bytes 294916

commit v2 on v1

--- a/solution.py
+++ b/solution.py
@@ -1,4 +1,3 @@
-import functools
 import math
 
 import jax
@@ -35,8 +34,8 @@
 
 
 def kernel(
-    meta, capcol, q_hbm, g_hbm, cache_hbm, kw_hbm, vw_hbm,
-    qg_hbm, text_ref, parts_hbm,
+    slots_s, tiles_s, slots_v, q_hbm, g_hbm, cache_hbm, kw_hbm, vw_hbm,
+    qg_hbm, text_ref, parts_hbm, crowded,
     q_v, g_v, raw, kvp, w_v, qg_v, ds_s, at_s, parts, prx, pm, yrx, x_s, tsend, xrx, town, zsend, zrx,
     load_sem, store_sem, ps, pr, ys, yr, xs, xr, zs, zr,
 ):
@@ -71,6 +70,26 @@
     partners = [pair_id] + y_ids + x_ids + z_ids
     for partner in partners:
         pl.semaphore_signal(barrier, inc=1, device_id=partner, device_id_type=MESH)
+
+    base = (seq // GROUP) * GROUP
+    near = [slots_s[s, base + j] for j in range(GROUP) for s in range(2)]
+    low, high = CAPS, -1
+    for c in near:
+        low = jnp.minimum(low, c)
+        high = jnp.maximum(high, jnp.where(c < CAPS, c, -1))
+    extra = 0
+    for c in near:
+        extra = extra + jnp.where((c < CAPS) & (c != low) & (c != high), 1, 0)
+    rank = [
+        jnp.where(extra == 0, jnp.where(slots_s[s, seq] != low, 1, 0), s) for s in range(2)
+    ]
+    weights = [
+        [
+            sum(jnp.where(rank[s] == r, tiles_s[s, t], 0) for s in range(2)).astype(F32)
+            for r in range(2)
+        ]
+        for t in range(NT)
+    ]
 
     n = lax.broadcasted_iota(jnp.int32, (L, L), 0)
     place = (n >> 2) & (NZ - 1)
@@ -119,7 +138,7 @@
     def attend(h, t):
         rows = slice(t * TILE, (t + 1) * TILE)
         cols = slice(h * DH, (h + 1) * DH)
-        kv = kvp[meta[t], h]
+        kv = kvp[tiles_s[1, t], h]
         q = q_v[rows, cols]
         g = g_v[rows, cols]
         zero = jnp.zeros_like(q)
@@ -143,7 +162,7 @@
         tiles = []
         for t in range(NT):
             v = ref[t * TILE : (t + 1) * TILE, h * DH : (h + 1) * DH].astype(F32)
-            ranks = [v * meta[NT + 2 * t + r].astype(F32) for r in range(2)]
+            ranks = [v * weights[t][r] for r in range(2)]
             tiles.append(jnp.concatenate(ranks, axis=1).astype(BF16))
         return jnp.concatenate(tiles, axis=0)
 
@@ -225,9 +244,33 @@
                 z_copy(j, z).start()
     zrx[z] = zsend[NZ - 1]
 
+    lane = lax.broadcasted_iota(jnp.int32, (8, 128), 1)
+    slot = [jnp.broadcast_to(slots_v[s : s + 1, :], (8, 128)) for s in range(2)]
+
+    def over_group(pick, v):
+        for b in (1, 2):
+            other = jnp.where((lane & b) == 0, pltpu.roll(v, 128 - b, 1), pltpu.roll(v, b, 1))
+            v = pick(v, other)
+        return v
+
+    low = over_group(jnp.minimum, jnp.minimum(slot[0], slot[1]))
+    high = [jnp.where(v < CAPS, v, -1) for v in slot]
+    high = over_group(jnp.maximum, jnp.maximum(high[0], high[1]))
+    third = [jnp.where((v < CAPS) & (v != low) & (v != high), 1.0, 0.0) for v in slot]
+    crowded[0] = jnp.max(jnp.maximum(third[0], third[1])).astype(jnp.int32)
+    high = jnp.where(high > low, high, CAPS)
+    spread = one_hot(
+        lax.broadcasted_iota(jnp.int32, (128, 256), 0),
+        (lax.broadcasted_iota(jnp.int32, (128, 256), 1) >> 3) * GROUP,
+    )
+    low = jnp.dot(low.astype(F32).astype(BF16), spread, preferred_element_type=F32)
+    high = jnp.dot(high.astype(F32).astype(BF16), spread, preferred_element_type=F32)
+    second = (lax.broadcasted_iota(jnp.int32, (8, 256), 1) & 4) != 0
+    capcol = jnp.where(second, high, low)[0:1]
+
     rows = lax.broadcasted_iota(jnp.int32, (CAPS * ROWS, 256), 0)
     cols = lax.broadcasted_iota(jnp.int32, (CAPS * ROWS, 256), 1)
-    held = (capcol[...] == (rows >> 2)) & ((rows & 3) == (cols & 3))
+    held = (capcol == (rows >> 2).astype(F32)) & ((rows & 3) == (cols & 3))
     select = jnp.where(held, 1.0, 0.0).astype(BF16)
     for j in range(NZ - 1):
         z_copy(j, lax.rem(z + NZ - ORDER[j], NZ)).wait_recv()
@@ -247,7 +290,7 @@
         store.wait()
 
 
-def run(meta, capcol, queries, out_grad, cache, key_weight, value_weight):
+def run(slots, tiles, queries, out_grad, cache, key_weight, value_weight):
     hbm = pl.BlockSpec(memory_space=pl.ANY)
     dma = pltpu.SemaphoreType.DMA
     return pl.pallas_call(
@@ -256,13 +299,20 @@
             jax.ShapeDtypeStruct((NT * TILE, HD), BF16),
             jax.ShapeDtypeStruct((CAPS * ROWS, HD), BF16),
             jax.ShapeDtypeStruct((NH, 2, 2, 256, 256), BF16),
+            jax.ShapeDtypeStruct((1,), jnp.int32),
         ),
         in_specs=[
+            pl.BlockSpec(memory_space=pltpu.SMEM),
             pl.BlockSpec(memory_space=pltpu.SMEM),
             pl.BlockSpec(memory_space=pltpu.VMEM),
             hbm, hbm, hbm, hbm, hbm,
         ],
-        out_specs=(hbm, pl.BlockSpec(memory_space=pltpu.VMEM), hbm),
+        out_specs=(
+            hbm,
+            pl.BlockSpec(memory_space=pltpu.VMEM),
+            hbm,
+            pl.BlockSpec(memory_space=pltpu.SMEM),
+        ),
         scratch_shapes=[
             pltpu.VMEM((NT * TILE, HD), BF16),
             pltpu.VMEM((NT * TILE, HD), BF16),
@@ -294,10 +344,10 @@
             dma((NZ - 1,)),
         ],
         compiler_params=pltpu.CompilerParams(
-            collective_id=0, has_side_effects=True, vmem_limit_bytes=48 * 1024 * 1024
+            collective_id=0, has_side_effects=True, vmem_limit_bytes=67043328
         ),
     )(
-        meta, capcol, queries, out_grad, cache,
+        slots, tiles, slots, queries, out_grad, cache,
         key_weight.reshape(NX, HD, HD), value_weight.reshape(NX, HD, HD),
     )
 
@@ -310,7 +360,12 @@
     split = parts.reshape(NH, 2, 2, NY, NZ, ROWS, 2, DH)[:, :, :, :, order]
     outgoing = split.transpose(4, 3, 1, 6, 5, 2, 0, 7).reshape(2 * NY * NZ, 2, ROWS * 2 * HD)
     received = lax.all_to_all(outgoing, "seq", split_axis=0, concat_axis=0, tiled=True)
-    table = slot_caption.reshape(1, -1)
+    groups = slot_caption.reshape(-1, GROUP * 2)
+    low = jnp.min(groups, axis=1, keepdims=True)
+    high = jnp.max(jnp.where(groups < CAPS, groups, -1), axis=1, keepdims=True)
+    fits = jnp.all((groups == CAPS) | (groups == low) | (groups == high), axis=1, keepdims=True)
+    ranks = jnp.concatenate([low, jnp.where(high > low, high, CAPS)], axis=1)
+    table = jnp.where(fits, jnp.tile(ranks, (1, GROUP)), groups).reshape(1, -1)
     selector = (table == jnp.arange(CAPS, dtype=jnp.int32)[:, None]).astype(BF16)
     summed = jnp.dot(selector, received.reshape(-1, ROWS * 2 * HD), preferred_element_type=F32)
     summed = summed.reshape(CAPS * ROWS, 2, HD)
@@ -323,25 +378,11 @@
 
 
 def shards(queries, out_grad, tile_mask, slot_caption, caption_cache, key_weight, value_weight):
-    me = lax.axis_index("seq")
-    groups = slot_caption.reshape(-1, GROUP * 2)
-    live = groups < CAPS
-    low = jnp.min(jnp.where(live, groups, CAPS), axis=1)
-    high = jnp.max(jnp.where(live, groups, -1), axis=1)
-    fits = jnp.all(~live | (groups == low[:, None]) | (groups == high[:, None]))
-    held = jnp.stack([low, jnp.where(high > low, high, CAPS)], axis=1)
-    capcol = jnp.repeat(held.reshape(1, -1), ROWS, axis=1)
-    mine = lax.dynamic_slice(slot_caption, (me, 0), (1, 2))[0]
-    rank = jnp.where(fits, (mine != low[me // GROUP]).astype(jnp.int32), jnp.arange(2, dtype=jnp.int32))
-    mask = jnp.sum(
-        tile_mask[:, :, None] * (rank[:, None] == jnp.arange(2, dtype=jnp.int32)[None, :]), axis=1
-    )
-    meta = jnp.concatenate([tile_mask[:, 1], mask.reshape(-1)]).astype(jnp.int32)
-    query_grad, fast, parts = run(
-        meta, capcol, queries, out_grad, caption_cache, key_weight, value_weight
+    query_grad, fast, parts, crowded = run(
+        slot_caption.T, tile_mask.T, queries, out_grad, caption_cache, key_weight, value_weight
     )
     text = lax.cond(
-        fits,
+        crowded[0] == 0,
         lambda f, p, s, k, v: f,
         lambda f, p, s, k, v: general(p, s, k, v),
         fast, parts, slot_caption, key_weight, value_weight,

time: 65.2 us -> 54.2 us (0.83)
  other arithmetic: 5.34 us -> 0 us
  local copies, waits for them, and re-layouts: 6.49 us -> 1.66 us
    unnamed x11 -> x5, local copies, waits for them, and re-layouts: 4.07 us -> 0.74 us
    convert_element_type x2 -> x0, other arithmetic: 1.58 us -> none  [the longest x1 1.51 us: shards(): (mine != low[me // GROUP]).astype(jnp.int32)]
    reduce_and x1 -> x0, other arithmetic: 1.33 us -> none  [shards(): fits = jnp.all(~live | (groups == low[:, None]) | (groups == high[:, None]))]
    reshape x1, local copies, waits for them, and re-layouts: 0.03 us -> 0.92 us  [shards(): return (query_grad, text.reshape(CAPS, ROWS, HD))]
    reduce_max x2 -> x0, other arithmetic: 0.82 us -> none  [shards(): high = jnp.max(jnp.where(live, groups, -1), axis=1)]
    reduce_sum x1 -> x0, other arithmetic: 0.76 us -> none  [shards(): jnp.sum(tile_mask[:, :, None] * (rank[:, None] == jnp.arange(2, dtype=jnp...]
    squeeze x1 -> x0, local copies, waits for them, and re-layouts: 0.68 us -> none  [shards(): tile_mask[:, 1]]
where the time goes in v2:
time: 54.2 us; the launch traced here: 54 us
  Pallas kernels  50.8 us (94%)
  local copies, waits for them, and re-layouts  1.66 us (3%)
  between operations  1.27 us (2%)
    pallas_call x1, Pallas kernels, run(): pl.pallas_call(kernel, out_shape=(jax.ShapeDtypeStruct((NT * TILE, HD), B...  50.8 us

profile of v2, /device:TPU:1, one launch (start us, length us, event | category | flops | bytes accessed | tf_op | source)
XLA Modules:
  0.0 54.0 jit_solution(14181752673637269)
XLA Ops:
  0.6 50.8 %shard_map.96 = (bf16[384,384]{1,0:T(8,128)(2,1)}, bf16[128,384]{1,0:T(8,128)(2,1)}, bf16[3,2,2,256,256]{4,3,2,1,0:T(8,128)(2,1)}, s32[1]{0:T(128)}) custom-call(s32[2,128]{1,0:T(2,128)} %bitcast.33, s32[2,3]{1,0:T(2,128)} %bitcast.36, s32[2,128]{1,0:T(2,128)} %bitcast.34, bf16[384,384]{1,0:T(8,128)(2,1)} %q_hbm.1, bf16[384,384]{1,0:T(8,128)(2,1)} %g_hbm.1, ...), custom_call_target="tpu_custom_call" | custom-call | tf_op jit(solution)/shard_map/pallas_call | solution.py:296
  52.1 0.0 copy-start.2
  52.1 1.2 %conditional.1 = (bf16[32,4,384]{2,1,0:T(4,128)(2,1)S(1)}) conditional(s32[]{:T(128)} %bitcast.8, (s32[128,2]{0,1:T(2,128)}, bf16[3,2,2,256,256]{4,3,2,1,0:T(8,128)(2,1)}, (), bf16[1536,384]{1,0:T(8,128)(2,1)}, bf16[1536,384]{1,0:T(8,128)(2,1)}) %tuple.16, bf16[128,384]{1,0:T(8,128)(2,1)} %get-tuple-element.31), branch_computations={%region_0.9_spmd, %region_9.10_spmd} | conditional | flops 1862627456 | bytes 45943780 | solution.py:384
  52.3 0.9 %reshape.82 = bf16[32,4,384]{2,1,0:T(4,128)(2,1)S(1)} reshape(bf16[128,384]{1,0:T(8,128)(2,1)} %param.1) | data formatting | bytes 196608 | tf_op jit(solution)/shard_map/reshape | solution.py:390
  53.2 0.0 copy-start.3
  53.2 0.0 copy-done.2
  53.3 0.7 %copy.48 = bf16[384,384]{1,0:T(8,128)(2,1)} copy(bf16[384,384]{1,0:T(8,128)(2,1)S(1)} %copy-done.2) | data formatting | bytes 589824
  54.0 0.0 copy-done.3
Async XLA Ops:
  52.1 1.2 %copy-start.2 = (bf16[384,384]{1,0:T(8,128)(2,1)S(1)}, bf16[384,384]{1,0:T(8,128)(2,1)}, u32[]{:S(2)}) copy-start(bf16[384,384]{1,0:T(8,128)(2,1)} %get-tuple-element.58) | copy-start | bytes 884740
  53.2 0.8 %copy-start.3 = (bf16[32,4,384]{2,1,0:T(4,128)(2,1)}, bf16[32,4,384]{2,1,0:T(4,128)(2,1)S(1)}, u32[]{:S(2)}) copy-start(bf16[32,4,384]{2,1,0:T(4,128)(2,1)S(1)} %get-tuple-element.60) | copy-start | bytes 294916

commit v3 on v0

v3 whole, which is shorter than its diff:
```python
import math

import jax
import jax.numpy as jnp
from jax import lax
from jax.experimental import pallas as pl
from jax.experimental.pallas import tpu as pltpu
from jax.sharding import PartitionSpec as P

DH = 128
L = 512
TILE = 128
NT = 3
NH = 3
NX = 4
NY = 4
NZ = 16
NC = 2
ROWS = 4
GROUP = 4
CAPS = 32
HD = NH * DH
HALF = 256
BLOCK = 64
STEP = 64
INV_ROOT = 1.0 / math.sqrt(DH)
MESH = pl.DeviceIdType.MESH
F32 = jnp.float32
BF16 = jnp.bfloat16
NT_DIMS = (((1,), (1,)), ((), ()))
TN_DIMS = (((0,), (0,)), ((), ()))
EXP_SCALE = INV_ROOT * math.log2(math.e)
ORDER = [4 + j // 2 if j % 2 == 0 else 4 - (j + 1) // 2 for j in range(NZ // 2)]


def one_hot(rows, columns):
    return jnp.where(rows == columns, 1.0, 0.0).astype(BF16)


def fold(pick, v):
    return pick(v.reshape(-1, 8, v.shape[-1]), axis=0)


def kernel(
    slots_s, tiles_s, slots_v, q_hbm, g_hbm, cache_hbm, kw_hbm, vw_hbm,
    qg_hbm, text_ref, parts_hbm, crowded,
    q_v, g_v, raw, w_v, qg_v, res_s, top_s, part_s, e_s, ds_s, at_s,
    parts, prx, pm, yax, ysum, ybx, ytx, x_s, t_s, xsend, xrx, zsend, zrx,
    load_sem, store_sem, ps, pr, yas, yar, ybs, ybr, ts, tr, xs, xr, zs, zr,
):
    seq = lax.axis_index("seq")
    x = lax.axis_index("head")
    core = lax.rem(seq, 2)
    y = lax.rem(seq // 2, NY)
    z = seq // (2 * NY)
    even = lax.rem(y, 2) == 0
    odd = lax.rem(core + z, 2)

    def at(z_, y_, core_):
        return ((lax.rem(z_ + NZ, NZ) * NY + lax.rem(y_, NY)) * 2 + core_, x)

    pair_id = at(z, y, 1 - core)
    mate = jnp.where(even, y + 1, y - 1)
    across = NY - 1 - y
    x_ids = [(seq, lax.rem(x + 1, NX)), (seq, lax.rem(x + NX - 1, NX))]

    loads = []
    for kv in range(2):
        for half in range(2):
            for b in range(NY):
                loads.append(
                    pltpu.make_async_copy(
                        cache_hbm.at[kv, :, :, half, b],
                        raw.at[kv, :, half, b],
                        load_sem.at[(kv * 2 + half) * NY + b],
                    )
                )
    n_cache = len(loads)
    for source, target in (
        (q_hbm, q_v), (g_hbm, g_v), (kw_hbm, w_v.at[0]), (vw_hbm, w_v.at[1])
    ):
        loads.append(pltpu.make_async_copy(source, target, load_sem.at[len(loads)]))
    for load in loads:
        load.start()

    barrier = pltpu.get_barrier_semaphore()
    sources = [pair_id]
    sources += [at(z, mate, core), at(z, across, core)]
    sources += x_ids
    sources += [at(z + 1, 0, core)]
    sources += [at(z + NZ - k, y, lax.rem(z, 2)) for k in range(1, NZ)]
    for source in sources:
        pl.semaphore_signal(barrier, inc=1, device_id=source, device_id_type=MESH)

    @pl.when(y != 2)
    def _():
        pl.semaphore_signal(
            barrier, inc=1, device_id=at(z, 2, core), device_id_type=MESH
        )

    tails = jnp.where(y == 0, NY, jnp.where(y == 2, NY - 1, 0))
    greetings = 5 + tails + NZ - 2 + 2 * odd

    base = (seq // GROUP) * GROUP
    before = lax.rem(base + slots_s.shape[1] - 1, slots_s.shape[1])
    own = jnp.minimum(slots_s[0, base + GROUP - 1], slots_s[1, base + GROUP - 1])
    prior = jnp.minimum(slots_s[0, before], slots_s[1, before])
    extra = 0
    for j in range(GROUP):
        for s in range(2):
            c = slots_s[s, base + j]
            out = (c < CAPS) & (c != own)
            if j < 2:
                out = out & (c != prior)
            extra = extra + jnp.where(out, 1, 0)
    rank = [
        jnp.where(extra == 0, jnp.where(slots_s[s, seq] != own, 1, 0), s) for s in range(2)
    ]
    weights = [
        [
            sum(jnp.where(rank[s] == r, tiles_s[s, t], 0) for s in range(2)).astype(F32)
            for r in range(2)
        ]
        for t in range(NT)
    ]

    def pair_copy(h, r):
        return pltpu.make_async_remote_copy(
            src_ref=parts.at[h, r, 1 - core], dst_ref=prx.at[h, r],
            send_sem=ps.at[h, r], recv_sem=pr.at[h, r],
            device_id=pair_id, device_id_type=MESH,
        )

    def mate_copy(h, i):
        block = NY - 1 - mate if i else mate
        return pltpu.make_async_remote_copy(
            src_ref=pm.at[h, 0, block], dst_ref=yax.at[h, i],
            send_sem=yas.at[h, i], recv_sem=yar.at[h, i],
            device_id=at(z, mate, core), device_id_type=MESH,
        )

    def across_copy(h):
        return pltpu.make_async_remote_copy(
            src_ref=ysum.at[h], dst_ref=ybx.at[h],
            send_sem=ybs.at[h], recv_sem=ybr.at[h],
            device_id=at(z, across, core), device_id_type=MESH,
        )

    def tail_copy(h, k, place):
        return pltpu.make_async_remote_copy(
            src_ref=pm.at[h, 1, lax.rem(y + k, NY)], dst_ref=ytx.at[h, place],
            send_sem=ts.at[h, k], recv_sem=tr.at[h, place],
            device_id=at(jnp.where(y == 0, z + NZ - 1, z), y + k, core), device_id_type=MESH,
        )

    def x_copy(d, m, c):
        return pltpu.make_async_remote_copy(
            src_ref=xsend.at[d, m, c], dst_ref=xrx.at[d, m, c],
            send_sem=xs.at[d, m, c], recv_sem=xr.at[d, m, c],
            device_id=x_ids[d], device_id_type=MESH,
        )

    def z_copy(j, other, source):
        c = 1 - core if other else core
        return pltpu.make_async_remote_copy(
            src_ref=zsend.at[2 * j + c], dst_ref=zrx.at[source],
            send_sem=zs.at[2 * j + other], recv_sem=zr.at[source],
            device_id=at(z + odd + 2 * ORDER[j], y, c), device_id_type=MESH,
        )

    def slot_block(h, t, kv):
        return raw[kv, tiles_s[1, t], :, :, :, :, h * DH : (h + 1) * DH].reshape(L, DH)

    def score(h, t):
        rows = slice(t * TILE, (t + 1) * TILE)
        cols = slice(h * DH, (h + 1) * DH)
        q = q_v[rows, cols]
        g = g_v[rows, cols]
        zero = jnp.zeros_like(q)
        both = jnp.concatenate(
            [jnp.concatenate([q, zero], axis=1), jnp.concatenate([zero, g], axis=1)], axis=0
        )
        res = lax.dot_general(
            jnp.concatenate([slot_block(h, t, 0), slot_block(h, t, 1)], axis=1),
            both, NT_DIMS, preferred_element_type=F32,
        )
        res_s[t] = res
        top_s[t] = fold(jnp.max, res[:, :TILE])

    def attend(h, t):
        rows = slice(t * TILE, (t + 1) * TILE)
        top = jnp.max(top_s[t], axis=0, keepdims=True)
        total = jnp.zeros((8, TILE), F32)
        dot = jnp.zeros((8, TILE), F32)
        for i in range(0, L, STEP):
            e = jnp.exp2((res_s[t, i : i + STEP, :TILE] - top) * EXP_SCALE)
            e_s[t, i : i + STEP] = e
            total = total + fold(jnp.sum, e)
            dot = dot + fold(jnp.sum, e * res_s[t, i : i + STEP, TILE:])
        inverse = 1.0 / jnp.sum(total, axis=0, keepdims=True)
        row_dot = jnp.sum(dot, axis=0, keepdims=True) * inverse
        for i in range(0, L, STEP):
            att = e_s[t, i : i + STEP] * inverse
            at_s[h, i : i + STEP, rows] = att.astype(BF16)
            ds_s[h, i : i + STEP, rows] = (
                att * (res_s[t, i : i + STEP, TILE:] - row_dot)
            ).astype(BF16)

    def query(h, t):
        rows = slice(t * TILE, (t + 1) * TILE)
        qg = lax.dot_general(
            ds_s[h, :, rows], slot_block(h, t, 0), TN_DIMS, preferred_element_type=F32
        )
        qg_v[rows, h * DH : (h + 1) * DH] = (qg * INV_ROOT).astype(BF16)

    def masked(ref, h, t):
        v = ref[t * TILE : (t + 1) * TILE, h * DH : (h + 1) * DH].astype(F32)
        return jnp.concatenate([v * weights[t][r] for r in range(2)], axis=1).astype(BF16)

    def reduce_first(h, kv):
        lhs, rhs = ((ds_s, q_v), (at_s, g_v))[kv]
        tiles = jnp.concatenate([masked(rhs, h, 0), masked(rhs, h, 1)], axis=0)
        part_s[kv] = jnp.dot(lhs[h, :, : 2 * TILE], tiles, preferred_element_type=F32)

    def reduce_last(h, kv):
        lhs, rhs = ((ds_s, q_v), (at_s, g_v))[kv]
        part = part_s[kv] + jnp.dot(
            lhs[h, :, 2 * TILE :], masked(rhs, h, 2), preferred_element_type=F32
        )
        if kv == 0:
            part = part * INV_ROOT
        for r in range(2):
            for half in range(2):
                parts[h, r, half, kv] = part[
                    half * HALF : (half + 1) * HALF, r * DH : (r + 1) * DH
                ].astype(BF16)

    def add_pair(h, r):
        pair_copy(h, r).wait_recv()
        total = (parts[h, r, core].astype(F32) + prx[h, r].astype(F32)).astype(BF16)
        for b in range(NY):
            pm[h, r, b] = total[:, b * BLOCK : (b + 1) * BLOCK, :]

    def merge_pair(h):
        add_pair(h, 0)
        for i in (1, 0):
            mate_copy(h, i).start()

        @pl.when(even)
        def _():
            add_pair(h, 1)
            for k in (2, 1, 3):
                tail_copy(h, k, y // 2).start()

            @pl.when(y == 0)
            def _():
                tail_copy(h, 0, y // 2).start()

            @pl.when(y != 0)
            def _():
                ytx[h, 1] = pm[h, 1, y]

    def join_group(h):
        mate_copy(h, 1).wait_recv()
        ysum[h] = (pm[h, 0, across].astype(F32) + yax[h, 1].astype(F32)).astype(BF16)
        across_copy(h).start()

    for load in loads[: n_cache + 2]:
        load.wait()
    stores = []
    score(0, 0)
    for h in range(NH):
        score(h, 1)
        attend(h, 0)
        score(h, 2)
        attend(h, 1)
        if h > 1:
            join_group(h - 2)
        if h > 0:
            merge_pair(h - 1)
        if h + 1 < NH:
            score(h + 1, 0)
        reduce_first(h, 1)
        reduce_first(h, 0)
        attend(h, 2)
        reduce_last(h, 1)
        reduce_last(h, 0)
        if h == 0:
            pl.semaphore_wait(barrier, greetings)
        pair_copy(h, 0).start()

        @pl.when(even)
        def _(h=h):
            pair_copy(h, 1).start()

        store = pltpu.make_async_copy(parts.at[h], parts_hbm.at[h], store_sem.at[h])
        store.start()
        stores.append(store)
    for h in range(NH - 1):
        for t in range(NT):
            query(h, t)
        if h == 0:
            join_group(NH - 2)
    merge_pair(NH - 1)
    for t in range(NT):
        query(NH - 1, t)
    store = pltpu.make_async_copy(qg_v, qg_hbm, store_sem.at[NH])
    store.start()
    stores.append(store)

    lane = lax.broadcasted_iota(jnp.int32, (8, 128), 1)
    spot = lane & (GROUP - 1)
    slot = [jnp.broadcast_to(slots_v[s : s + 1, :], (8, 128)) for s in range(2)]
    lowest = jnp.minimum(slot[0], slot[1])
    owner, earlier = lowest, lowest
    for j in range(GROUP - 1):
        owner = jnp.where(spot == j, pltpu.roll(lowest, 128 - (GROUP - 1 - j), 1), owner)
    for j in range(2):
        earlier = jnp.where(spot == j, pltpu.roll(lowest, j + 1, 1), earlier)
    third = [
        jnp.where((v < CAPS) & (v != owner) & ((v != earlier) | (spot >= 2)), 1.0, 0.0)
        for v in slot
    ]
    crowded[0] = jnp.max(jnp.maximum(third[0], third[1])).astype(jnp.int32)
    rows = lax.broadcasted_iota(jnp.int32, (CAPS * ROWS, 128), 0)
    cols = lax.broadcasted_iota(jnp.int32, (CAPS * ROWS, 128), 1)
    held = (owner[0:1] == (rows >> 2)) & ((rows & 3) == (cols & 3))
    select = jnp.where(held, 1.0, 0.0).astype(BF16)

    place = rows >> 4
    step = jnp.where((place & 1) == 0, 4 + (place >> 1), 3 - (place >> 1))
    dest = (z + odd + 2 * step) & (NZ - 1)
    old = ((rows >> 2) & 1) * BLOCK + (dest >> 1) * 8 + ((rows >> 3) & 1) * 4 + (rows & 3)
    perm = one_hot(old, cols)

    loads[n_cache + 2].wait()
    loads[n_cache + 3].wait()
    join_group(NH - 1)
    mine = y // 2
    for h in range(NH):
        tail_copy(h, 0, 0).wait_recv()

        @pl.when(y != 2)
        def _(h=h):
            tail_copy(h, 0, 1).wait_recv()

        mate_copy(h, 0).wait_recv()
        near = pm[h, 0, y].astype(F32) + yax[h, 0].astype(F32) + ytx[h, 1 - mine].astype(F32)
        across_copy(h).wait_recv()
        far = ybx[h].astype(F32) + ytx[h, mine].astype(F32)
        for kv in range(2):
            cols = slice(kv * HD + h * DH, kv * HD + (h + 1) * DH)
            x_s[mine, :, cols] = near[kv].astype(BF16)
            x_s[1 - mine, :, cols] = far[kv].astype(BF16)
    joined = jnp.dot(
        perm, x_s[...].reshape(2 * BLOCK, 2 * HD), preferred_element_type=F32
    ).astype(BF16)
    chunk = 2 * BLOCK // NC
    places = NZ // 2 // NC

    def project(target):
        return lax.dot_general(
            joined[:, :HD], w_v[0, target], NT_DIMS, preferred_element_type=F32
        ) + lax.dot_general(joined[:, HD:], w_v[1, target], NT_DIMS, preferred_element_type=F32)

    def half(c, d):
        start = c * chunk + d * (chunk // 2)
        return slice(start, start + chunk // 2)

    piece = project(lax.rem(x + 2, NX))
    for c in range(NC):
        for d in range(2):
            xsend[d, 0, c] = piece[half(c, d)].astype(BF16)
            x_copy(d, 0, c).start()
    for d in range(2):
        piece = project(lax.rem(x + (1, NX - 1)[d], NX))
        t_s[d] = piece
        for c in range(NC):
            xsend[d, 1, c] = piece[half(c, 1 - d)].astype(BF16)
            x_copy(d, 1, c).start()
    t_s[2] = project(x)
    for c in range(NC):
        for d in range(2):
            x_copy(d, 0, c).wait_recv()
            xsend[d, 2, c] = (t_s[d, half(c, d)] + xrx[d, 0, c].astype(F32)).astype(BF16)
            x_copy(d, 2, c).start()
    for c in range(NC):
        total = []
        for d in range(2):
            x_copy(1 - d, 1, c).wait_recv()
            x_copy(d, 2, c).wait_recv()
            total.append(
                t_s[2, half(c, d)] + xrx[1 - d, 1, c].astype(F32) + xrx[d, 2, c].astype(F32)
            )
        total = jnp.concatenate(total, axis=0)
        zsend[2 * c * places : 2 * (c + 1) * places] = total.reshape(2 * places, 8, HD).astype(BF16)
        for j in range(c * places, (c + 1) * places):
            z_copy(j, 1, z).start()
            if ORDER[j] > 0:
                z_copy(j, 0, z).start()
            else:

                @pl.when(odd == 1)
                def _(j=j):
                    z_copy(j, 0, z).start()

                @pl.when(odd == 0)
                def _(j=j):
                    zrx[z] = zsend[2 * j + core]

    for k in range(1, NZ):
        z_copy(0, 0, lax.rem(z + NZ - k, NZ)).wait_recv()

    @pl.when(odd == 1)
    def _():
        z_copy(0, 0, z).wait_recv()

    text = jnp.dot(select, zrx[...].reshape(128, HD), preferred_element_type=F32)
    text_ref[...] = text.astype(BF16)

    for h in range(NH):
        pair_copy(h, 0).wait_send()
        for i in range(2):
            mate_copy(h, i).wait_send()
        across_copy(h).wait_send()

        @pl.when(even)
        def _(h=h):
            pair_copy(h, 1).wait_send()
            for k in range(1, NY):
                tail_copy(h, k, y // 2).wait_send()

            @pl.when(y == 0)
            def _():
                tail_copy(h, 0, y // 2).wait_send()

    for c in range(NC):
        for d in range(2):
            for m in range(3):
                x_copy(d, m, c).wait_send()
    for j in range(NZ // 2):
        z_copy(j, 1, z).wait_send()
        if ORDER[j] > 0:
            z_copy(j, 0, z).wait_send()

    @pl.when(odd == 1)
    def _():
        z_copy(ORDER.index(0), 0, z).wait_send()

    for store in stores:
        store.wait()


def run(slots, tiles, queries, out_grad, cache, key_weight, value_weight):
    hbm = pl.BlockSpec(memory_space=pltpu.HBM)
    smem = pl.BlockSpec(memory_space=pltpu.SMEM)
    vmem = pl.BlockSpec(memory_space=pltpu.VMEM)
    dma = pltpu.SemaphoreType.DMA
    return pl.pallas_call(
        kernel,
        out_shape=(
            jax.ShapeDtypeStruct((NT * TILE, HD), BF16),
            jax.ShapeDtypeStruct((CAPS * ROWS, HD), BF16),
            jax.ShapeDtypeStruct((NH, 2, 2, 2, HALF, DH), BF16),
            jax.ShapeDtypeStruct((1,), jnp.int32),
        ),
        in_specs=[smem, smem, vmem, hbm, hbm, hbm, hbm, hbm],
        out_specs=(pl.BlockSpec(memory_space=pl.ANY), vmem, hbm, smem),
        scratch_shapes=[
            pltpu.VMEM((NT * TILE, HD), BF16),
            pltpu.VMEM((NT * TILE, HD), BF16),
            pltpu.VMEM((2, 2, 2, NY, NZ // 2, 8, HD), BF16),
            pltpu.VMEM((2, NX, HD, HD), BF16),
            pltpu.VMEM((NT * TILE, HD), BF16),
            pltpu.VMEM((NT, L, 2 * TILE), F32),
            pltpu.VMEM((NT, 8, TILE), F32),
            pltpu.VMEM((2, L, 2 * DH), F32),
            pltpu.VMEM((NT, L, TILE), F32),
            pltpu.VMEM((NH, L, NT * TILE), BF16),
            pltpu.VMEM((NH, L, NT * TILE), BF16),
            pltpu.VMEM((NH, 2, 2, 2, HALF, DH), BF16),
            pltpu.VMEM((NH, 2, 2, HALF, DH), BF16),
            pltpu.VMEM((NH, 2, NY, 2, BLOCK, DH), BF16),
            pltpu.VMEM((NH, 2, 2, BLOCK, DH), BF16),
            pltpu.VMEM((NH, 2, BLOCK, DH), BF16),
            pltpu.VMEM((NH, 2, BLOCK, DH), BF16),
            pltpu.VMEM((NH, 2, 2, BLOCK, DH), BF16),
            pltpu.VMEM((2, BLOCK, 2 * HD), BF16),
            pltpu.VMEM((3, 2 * BLOCK, HD), F32),
            pltpu.VMEM((2, 3, NC, BLOCK // NC, HD), BF16),
            pltpu.VMEM((2, 3, NC, BLOCK // NC, HD), BF16),
            pltpu.VMEM((NZ, 8, HD), BF16),
            pltpu.VMEM((NZ, 8, HD), BF16),
            dma((20,)),
            dma((NH + 1,)),
            dma((NH, 2)),
            dma((NH, 2)),
            dma((NH, 2)),
            dma((NH, 2)),
            dma((NH,)),
            dma((NH,)),
            dma((NH, NY)),
            dma((NH, 2)),
            dma((2, 3, NC)),
            dma((2, 3, NC)),
            dma((NZ,)),
            dma((NZ,)),
        ],
        compiler_params=pltpu.CompilerParams(
            collective_id=0, has_side_effects=True, vmem_limit_bytes=67043328
        ),
    )(
        slots, tiles, slots, queries, out_grad,
        cache.reshape(2, 2, NZ // 2, 2, NY, 8, HD),
        key_weight.reshape(NX, HD, HD), value_weight.reshape(NX, HD, HD),
    )


def general(parts, slot_caption, key_weight, value_weight):
    split = parts.reshape(NH, 2, 2, 2, NY, NZ // 2, 2, ROWS, DH)
    outgoing = split.transpose(5, 2, 4, 6, 1, 7, 3, 0, 8).reshape(-1, 2, ROWS * 2 * HD)
    received = lax.all_to_all(outgoing, "seq", split_axis=0, concat_axis=0, tiled=True)
    groups = slot_caption.reshape(-1, GROUP * 2)
    owner = jnp.min(groups[:, -2:], axis=1, keepdims=True)
    earlier = jnp.roll(owner, 1, axis=0)
    early = jnp.arange(GROUP * 2)[None, :] < 4
    fits = jnp.all(
        (groups == CAPS) | (groups == owner) | ((groups == earlier) & early), axis=1, keepdims=True
    )
    ranks = jnp.concatenate([owner, earlier], axis=1)
    table = jnp.where(fits, jnp.tile(ranks, (1, GROUP)), groups).reshape(1, -1)
    selector = (table == jnp.arange(CAPS, dtype=jnp.int32)[:, None]).astype(BF16)
    summed = jnp.dot(selector, received.reshape(-1, ROWS * 2 * HD), preferred_element_type=F32)
    summed = summed.reshape(CAPS * ROWS, 2, HD)
    highest = lax.Precision.HIGHEST
    text = jnp.einsum("mc,dc->md", summed[:, 0], key_weight.astype(F32), precision=highest)
    text = text + jnp.einsum("mc,dc->md", summed[:, 1], value_weight.astype(F32), precision=highest)
    pieces = text.reshape(CAPS * ROWS, NX, HD).transpose(1, 0, 2)
    pieces = lax.all_to_all(pieces, "head", split_axis=0, concat_axis=0, tiled=True)
    return jnp.sum(pieces, axis=0).astype(BF16)


def shards(queries, out_grad, tile_mask, slot_caption, caption_cache, key_weight, value_weight):
    query_grad, fast, parts, crowded = run(
        slot_caption.T, tile_mask.T, queries, out_grad, caption_cache, key_weight, value_weight
    )
    text = lax.cond(
        crowded[0] == 0,
        lambda f, p, s, k, v: f,
        lambda f, p, s, k, v: general(p, s, k, v),
        fast, parts, slot_caption, key_weight, value_weight,
    )
    return query_grad, text.reshape(CAPS, ROWS, HD)


def solution(mesh):
    placed = (
        P("seq", "head"),
        P("seq", "head"),
        P("seq", None),
        P(),
        P(None, "seq", None, "head"),
        P(None, "head"),
        P(None, "head"),
    )
    return jax.shard_map(
        shards,
        mesh=mesh,
        in_specs=placed,
        out_specs=(P("seq", "head"), P(None, "seq", "head")),
        check_vma=False,
    )
```

time: 437 us -> 51.5 us (0.12)
  blocking collectives: 297 us -> 0 us
  matrix products: 51.9 us -> 0 us
  Pallas kernels: 0 us -> 47.2 us
  local copies, waits for them, and re-layouts: 48.6 us -> 2.67 us
  waiting for transfers between devices: 20.3 us -> 0 us
  between operations: 14.2 us -> 1.25 us
    all_to_all x1 -> x0, blocking collectives: 297 us -> none  [shards(): lax.all_to_all(outgoing, 'seq', split_axis=1, concat_axis=1, tiled=True)]
    dot_general x13 -> x0, matrix products: 51.9 us -> none  [the longest x1 9.46 us: shards(): jnp.einsum('ts,tjhe->sjhe', slot_onehot, value_pieces, precision=highest)]
    pallas_call x0 -> x1, Pallas kernels: none -> 47.2 us  [run(): pl.pallas_call(kernel, out_shape=(jax.ShapeDtypeStruct((NT * TILE, HD), B...]
    reduce_scatter x1 -> x0, waiting for transfers between devices: 20.3 us -> none  [shards(): lax.psum_scatter(summed, 'head', scatter_dimension=2, tiled=True)]
    reshape x5 -> x1, local copies, waits for them, and re-layouts: 16.3 us -> 0.92 us  [shards(): return (query_grad, text.reshape(CAPS, ROWS, HD))]
    convert_element_type x5 -> x0, local copies, waits for them, and re-layouts: 14 us -> none  [the longest x1 3.75 us: shards(): key_part = key_part.astype(jnp.bfloat16).reshape(slot_count, L, width)]
    unnamed x25 -> x3, local copies, waits for them, and re-layouts: 9.05 us -> 1.75 us
    dot_general x1 -> x0, local copies, waits for them, and re-layouts: 6.61 us -> none  [shards(): jnp.dot(selector, received.reshape(slot_count * seq_count, block_rows * D...]
  transfers between devices with their start and end apart: 1 -> 0, of which waited for: 1 -> 0; matrix products, arithmetic and copies ran while one was open for 1% -> 0% of each run, Pallas kernels for 0% -> 0%
where the time goes in v3:
time: 51.5 us; the launch traced here: 51.3 us
  Pallas kernels  47.2 us (92%)
  local copies, waits for them, and re-layouts  2.67 us (5%)
  between operations  1.25 us (2%)
    pallas_call x1, Pallas kernels, run(): pl.pallas_call(kernel, out_shape=(jax.ShapeDtypeStruct((NT * TILE, HD), B...  47.2 us
    unnamed x3, local copies, waits for them, and re-layouts  1.75 us

profile of v3, /device:TPU:1, one launch (start us, length us, event | category | flops | bytes accessed | tf_op | source)
XLA Modules:
  0.0 51.3 jit_solution(1207647209215811485)
XLA Ops:
  0.6 47.2 %shard_map.86 = (bf16[384,384]{1,0:T(8,128)(2,1)}, bf16[128,384]{1,0:T(8,128)(2,1)}, bf16[3,2,2,2,256,128]{5,4,3,2,1,0:T(8,128)(2,1)}, s32[1]{0:T(128)}) custom-call(s32[2,128]{1,0:T(2,128)} %bitcast.43, s32[2,3]{1,0:T(2,128)} %bitcast.46, s32[2,128]{1,0:T(2,128)} %bitcast.44, bf16[384,384]{1,0:T(8,128)(2,1)} %q_hbm.1, bf16[384,384]{1,0:T(8,128)(2,1)} %g_hbm.1, ...), custom_call_target="tpu_custom_call" | custom-call | tf_op jit(solution)/shard_map/pallas_call | solution.py:459
  48.4 1.2 %conditional.1 = (bf16[32,4,384]{2,1,0:T(4,128)(2,1)S(1)}) conditional(s32[]{:T(128)} %bitcast.12, (s32[128,2]{0,1:T(2,128)}, bf16[3,2,2,2,256,128]{5,4,3,2,1,0:T(8,128)(2,1)}, bf16[1536,384]{1,0:T(8,128)(2,1)}, bf16[1536,384]{1,0:T(8,128)(2,1)}) %tuple.16, bf16[128,384]{1,0:T(8,128)(2,1)} %get-tuple-element.27), branch_computations={%region_0.5_spmd, %region_5.6_spmd} | conditional | flops 1862625536 | bytes 39644240 | solution.py:547
  48.6 0.9 %reshape.77 = bf16[32,4,384]{2,1,0:T(4,128)(2,1)S(1)} reshape(bf16[128,384]{1,0:T(8,128)(2,1)} %param.1) | data formatting | bytes 196608 | tf_op jit(solution)/shard_map/reshape | solution.py:553
  49.6 0.0 copy-start.2
  49.6 1.7 %copy.49 = bf16[384,384]{1,0:T(8,128)(2,1)} copy(bf16[384,384]{1,0:T(8,128)(2,1)} %get-tuple-element.32) | data formatting | bytes 589824
  51.3 0.0 copy-done.2
Async XLA Ops:
  49.6 1.8 %copy-start.2 = (bf16[32,4,384]{2,1,0:T(4,128)(2,1)}, bf16[32,4,384]{2,1,0:T(4,128)(2,1)S(1)}, u32[]{:S(2)}) copy-start(bf16[32,4,384]{2,1,0:T(4,128)(2,1)S(1)} %get-tuple-element.34) | copy-start | bytes 294916
